TPU v7x, 32 devices: a whole 2x2x4 slice. The times are simulated.
32 devices in a mesh: shard: 2 (over x), ctx: 4 (over z), tp: 4 (over y, core).
Axes of the slice: x: 2, y: 2, z: 4, core: 2. Of those that a mesh axis runs over, the one named last changes fastest.
Arguments:
- x_img: bfloat16 [6, 1024, 1536], P('shard', ('ctx', 'tp')), may hold values from -6 to 6
- x_txt: bfloat16 [6, 160, 1536], P('shard', ('ctx', 'tp')), may hold values from -6 to 6
- cond: bfloat16 [6, 1536], P('shard'), may hold values from -6 to 6
- lengths: int32 [6], P('shard'), may hold values from 77 to 154, as said below
- mod_w: bfloat16 [2, 1536, 6, 1536], P(None, ('shard', 'ctx'), None, 'tp'), may hold values from -0.15625 to 0.15625
- qkv_w: bfloat16 [2, 3, 1536, 1536], P(None, None, ('shard', 'ctx'), 'tp'), may hold values from -0.15625 to 0.15625
- o_w: bfloat16 [2, 1536, 1536], P(None, 'tp', ('shard', 'ctx')), may hold values from -0.875 to 0.875
- up_w: bfloat16 [2, 1536, 6144], P(None, ('shard', 'ctx'), 'tp'), may hold values from -0.15625 to 0.15625
- down_w: bfloat16 [2, 6144, 1536], P(None, 'tp', ('shard', 'ctx')), may hold values from -0.078125 to 0.078125
- norm_gain: float32 [2, 2, 64], replicated, may hold values from 1 to 1.6
- threshold: float32 [], replicated, may hold values from 1 to 2
- cot_img: bfloat16 [6, 1024, 1536], P('shard', ('ctx', 'tp')), may hold values from -6 to 6
- cot_txt: bfloat16 [6, 160, 1536], P('shard', ('ctx', 'tp')), may hold values from -6 to 6
Outputs:
- out_img: bfloat16 [6, 1024, 1536], P('shard', ('ctx', 'tp'))
- out_txt: bfloat16 [6, 160, 1536], P('shard', ('ctx', 'tp'))
- grad_img: float32 [6, 1024, 1536], P('shard', ('ctx', 'tp'))
- grad_txt: float32 [6, 160, 1536], P('shard', ('ctx', 'tp'))
- grad_cond: float32 [6, 1536], P('shard')
- grad_mod: float32 [2, 1536, 6, 1536], P(None, ('shard', 'ctx'), None, 'tp')
- grad_qkv: float32 [2, 3, 1536, 1536], P(None, None, ('shard', 'ctx'), 'tp')
- grad_o: float32 [2, 1536, 1536], P(None, 'tp', ('shard', 'ctx'))
- grad_up: float32 [2, 1536, 6144], P(None, ('shard', 'ctx'), 'tp')
- grad_down: float32 [2, 6144, 1536], P(None, 'tp', ('shard', 'ctx'))
- grad_gain: float32 [2, 2, 64], replicated
- clipped_qk: float32 [2, 2, 1536, 1536], P(None, None, ('shard', 'ctx'), 'tp')
- logit_peaks: float32 [24], P('tp')
Inputs may be any that keep to these rules, and one draw needn't show every extreme that they name: lengths: text tokens of a sequence; some sequence has exactly 154.
All inputs are finite; a program needn't handle non-finite values.
Results may differ from a plain program's by a relative error of at most 0.017.
Values may be sent and summed in bfloat16 or wider, within the bound.
No kernel may reach another device: no remote copies, remote signals or barrier semaphores. Data moves between devices by JAX's collectives and lax.ppermute only.
A program may use at most 256 MiB of HBM per device.

v0:
```python
import jax
import jax.numpy as jnp
from jax import lax
from jax.sharding import PartitionSpec as P

EPS = 1e-06
QUERY_SCALE = 0.125


def layer_norm(values):
    center = values - jnp.mean(values, axis=-1, keepdims=True)
    spread = jnp.mean(center * center, axis=-1, keepdims=True)
    return center * lax.rsqrt(spread + EPS)


def modulate(values, shift, scale):
    return layer_norm(values) * (1.0 + scale) + shift


def head_norm(values, gain_vec, factor):
    shape_in = values.shape
    split_heads = values.reshape(
        shape_in[:-1] + (shape_in[-1] // gain_vec.shape[0], gain_vec.shape[0])
    )
    square = jnp.mean(split_heads * split_heads, axis=-1, keepdims=True)
    return (split_heads * lax.rsqrt(square + EPS) * gain_vec * factor).reshape(shape_in)


def gelu_tanh(values):
    return jax.nn.gelu(values, approximate=True)


def gather_rows(first, second):
    return (
        lax.all_gather(first, "tp", axis=1, tiled=True),
        lax.all_gather(second, "tp", axis=1, tiled=True),
    )


def reduce_rows(first, second):
    return (
        lax.psum_scatter(first, "tp", scatter_dimension=1, tiled=True),
        lax.psum_scatter(second, "tp", scatter_dimension=1, tiled=True),
    )


def split_heads_major(values, head_dim):
    seq_count, row_count, columns = values.shape
    return values.reshape(seq_count, row_count, columns // head_dim, head_dim).transpose(2, 0, 1, 3)


def merge_heads(values):
    head_count, seq_count, row_count, head_dim = values.shape
    return values.transpose(1, 2, 0, 3).reshape(seq_count, row_count, head_count * head_dim)


def key_mask(lengths, img_member, txt_member, ctx_count):
    member_rows = img_member + txt_member
    key_place = jnp.arange(member_rows * ctx_count, dtype=jnp.int32)
    within = key_place % member_rows
    member = key_place // member_rows
    text_place = member * txt_member + within - img_member
    return (within < img_member)[None, :] | (text_place[None, :] < lengths[:, None])


def local(
    x_img,
    x_txt,
    cond,
    lengths,
    mod_w,
    qkv_w,
    o_w,
    up_w,
    down_w,
    norm_gain,
    threshold,
    cot_img,
    cot_txt,
):
    tp_count = lax.axis_size("tp")
    ctx_count = lax.axis_size("ctx")
    shard_count = lax.axis_size("shard")
    head_dim = norm_gain.shape[2]
    img_member = x_img.shape[1] * tp_count
    txt_member = x_txt.shape[1] * tp_count
    local_feat = mod_w.shape[3]
    owned_rows = mod_w.shape[1]
    gathered = (
        lax.all_gather(qkv_w, ("shard", "ctx"), axis=2, tiled=True),
        lax.all_gather(o_w, ("shard", "ctx"), axis=2, tiled=True),
        lax.all_gather(up_w, ("shard", "ctx"), axis=1, tiled=True),
        lax.all_gather(down_w, ("shard", "ctx"), axis=2, tiled=True),
    )
    qkv_all, out_all, up_all, down_all = gathered
    cond_float = cond.astype(jnp.float32)
    cond_act = jax.nn.silu(cond_float).astype(jnp.bfloat16)
    mod_all = lax.all_gather(mod_w, ("shard", "ctx"), axis=1, tiled=True)
    mod_local = jnp.einsum("sd,tdkf->tskf", cond_act, mod_all, preferred_element_type=jnp.float32)
    modulation = lax.all_gather(mod_local, "tp", axis=3, tiled=True)
    inputs = (x_img.astype(jnp.float32), x_txt.astype(jnp.float32))

    def entry(stream, index):
        return modulation[stream, :, index][:, None, :]

    first_low = [
        modulate(inputs[s], entry(s, 0), entry(s, 1)).astype(jnp.bfloat16) for s in range(2)
    ]
    first_in = gather_rows(first_low[0], first_low[1])
    projected = [
        jnp.einsum("srd,cdf->csrf", first_in[s], qkv_all[s], preferred_element_type=jnp.float32)
        for s in range(2)
    ]
    queries = jnp.concatenate(
        [head_norm(projected[s][0], norm_gain[s, 0], QUERY_SCALE) for s in range(2)], axis=1
    ).astype(jnp.bfloat16)
    keys_local = jnp.concatenate(
        [head_norm(projected[s][1], norm_gain[s, 1], 1.0) for s in range(2)], axis=1
    ).astype(jnp.bfloat16)
    values_local = jnp.concatenate([projected[s][2] for s in range(2)], axis=1).astype(jnp.bfloat16)
    keys_all, values_all = (
        lax.all_gather(keys_local, "ctx", axis=1, tiled=True),
        lax.all_gather(values_local, "ctx", axis=1, tiled=True),
    )
    key_masks = key_mask(lengths, img_member, txt_member, ctx_count)

    def attend_head(operands):
        query_head, key_head, value_head = operands
        scores = jnp.einsum(
            "sqd,skd->sqk", query_head, key_head, preferred_element_type=jnp.float32
        )
        masked = jnp.where(key_masks[:, None, :], scores, -jnp.inf)
        highest = jnp.max(masked, axis=-1, keepdims=True)
        weights_exp = jnp.exp(masked - highest)
        denominator = jnp.sum(weights_exp, axis=-1, keepdims=True)
        probabilities = (weights_exp / denominator).astype(jnp.bfloat16)
        mixed_out = jnp.einsum(
            "sqk,skd->sqd", probabilities, value_head, preferred_element_type=jnp.float32
        )
        return (
            mixed_out.astype(jnp.bfloat16),
            (highest + jnp.log(denominator))[..., 0],
            jnp.max(highest),
        )

    query_heads = split_heads_major(queries, head_dim)
    key_heads = split_heads_major(keys_all, head_dim)
    value_heads = split_heads_major(values_all, head_dim)
    attended, log_norm, head_peaks = lax.map(attend_head, (query_heads, key_heads, value_heads))
    peaks = lax.pmax(head_peaks, ("shard", "ctx"))
    attended = merge_heads(attended)
    segments = (attended[:, :img_member], attended[:, img_member:])
    attn_parts = [
        jnp.einsum("srf,fd->srd", segments[s], out_all[s], preferred_element_type=jnp.float32)
        for s in range(2)
    ]
    attn_out = reduce_rows(attn_parts[0], attn_parts[1])
    mid = [inputs[s] + entry(s, 2) * attn_out[s] for s in range(2)]
    second_low = [modulate(mid[s], entry(s, 3), entry(s, 4)).astype(jnp.bfloat16) for s in range(2)]
    second_in = gather_rows(second_low[0], second_low[1])
    hidden_pre = [
        jnp.einsum("srd,df->srf", second_in[s], up_all[s], preferred_element_type=jnp.float32)
        for s in range(2)
    ]
    hidden_low = [gelu_tanh(hidden_pre[s]).astype(jnp.bfloat16) for s in range(2)]
    mlp_parts = [
        jnp.einsum("srf,fd->srd", hidden_low[s], down_all[s], preferred_element_type=jnp.float32)
        for s in range(2)
    ]
    mlp_out = reduce_rows(mlp_parts[0], mlp_parts[1])
    results = [(mid[s] + entry(s, 5) * mlp_out[s]).astype(jnp.bfloat16) for s in range(2)]
    qkv_back, out_back, up_back, down_back = (
        lax.all_gather(qkv_w, ("shard", "ctx"), axis=2, tiled=True),
        lax.all_gather(o_w, ("shard", "ctx"), axis=2, tiled=True),
        lax.all_gather(up_w, ("shard", "ctx"), axis=1, tiled=True),
        lax.all_gather(down_w, ("shard", "ctx"), axis=2, tiled=True),
    )
    grad_out = (cot_img.astype(jnp.float32), cot_txt.astype(jnp.float32))
    mlp_grad_low = [(grad_out[s] * entry(s, 5)).astype(jnp.bfloat16) for s in range(2)]
    gate_two = [jnp.sum(grad_out[s] * mlp_out[s], axis=1) for s in range(2)]
    mlp_grad_in = gather_rows(mlp_grad_low[0], mlp_grad_low[1])
    grad_down = jnp.stack(
        [
            jnp.einsum(
                "srf,srd->fd", hidden_low[s], mlp_grad_in[s], preferred_element_type=jnp.float32
            )
            for s in range(2)
        ]
    )
    pre_grad = []
    for s in range(2):
        hidden_back = jnp.einsum(
            "srd,fd->srf", mlp_grad_in[s], down_back[s], preferred_element_type=jnp.float32
        )
        unused, gelu_vjp = jax.vjp(gelu_tanh, hidden_pre[s])
        pre_grad.append(gelu_vjp(hidden_back)[0].astype(jnp.bfloat16))
    grad_up = jnp.stack(
        [
            jnp.einsum("srd,srf->df", second_in[s], pre_grad[s], preferred_element_type=jnp.float32)
            for s in range(2)
        ]
    )
    second_parts = [
        jnp.einsum("srf,df->srd", pre_grad[s], up_back[s], preferred_element_type=jnp.float32)
        for s in range(2)
    ]
    second_grad = reduce_rows(second_parts[0], second_parts[1])
    mid_grad = []
    shift_two = []
    scale_two = []
    for s in range(2):
        unused, mod_vjp = jax.vjp(modulate, mid[s], entry(s, 3), entry(s, 4))
        mid_part, shift_part, scale_part = mod_vjp(second_grad[s])
        mid_grad.append(grad_out[s] + mid_part)
        shift_two.append(shift_part[:, 0])
        scale_two.append(scale_part[:, 0])
    attn_grad_low = [(mid_grad[s] * entry(s, 2)).astype(jnp.bfloat16) for s in range(2)]
    gate_one = [jnp.sum(mid_grad[s] * attn_out[s], axis=1) for s in range(2)]
    attn_grad_in = gather_rows(attn_grad_low[0], attn_grad_low[1])
    grad_outproj = jnp.stack(
        [
            jnp.einsum(
                "srf,srd->fd", segments[s], attn_grad_in[s], preferred_element_type=jnp.float32
            )
            for s in range(2)
        ]
    )
    mixed_grad = jnp.concatenate(
        [
            jnp.einsum(
                "srd,fd->srf", attn_grad_in[s], out_back[s], preferred_element_type=jnp.float32
            )
            for s in range(2)
        ],
        axis=1,
    ).astype(jnp.bfloat16)

    def attend_back(operands):
        query_head, key_head, value_head, grad_head, log_head = operands
        scores = jnp.einsum(
            "sqd,skd->sqk", query_head, key_head, preferred_element_type=jnp.float32
        )
        masked = jnp.where(key_masks[:, None, :], scores, -jnp.inf)
        probabilities = jnp.exp(masked - log_head[..., None])
        grad_prob = jnp.einsum(
            "sqd,skd->sqk", grad_head, value_head, preferred_element_type=jnp.float32
        )
        grad_score = (
            probabilities * (grad_prob - jnp.sum(probabilities * grad_prob, axis=-1, keepdims=True))
        ).astype(jnp.bfloat16)
        grad_query = jnp.einsum(
            "sqk,skd->sqd", grad_score, key_head, preferred_element_type=jnp.float32
        )
        grad_key = jnp.einsum(
            "sqk,sqd->skd", grad_score, query_head, preferred_element_type=jnp.float32
        )
        grad_value = jnp.einsum(
            "sqk,sqd->skd",
            probabilities.astype(jnp.bfloat16),
            grad_head,
            preferred_element_type=jnp.float32,
        )
        return (grad_query, grad_key, grad_value)

    query_grads, key_grads, value_grads = lax.map(
        attend_back,
        (query_heads, key_heads, value_heads, split_heads_major(mixed_grad, head_dim), log_norm),
    )
    key_sum, value_sum = (
        lax.psum_scatter(
            merge_heads(key_grads).astype(jnp.bfloat16), "ctx", scatter_dimension=1, tiled=True
        ).astype(jnp.float32),
        lax.psum_scatter(
            merge_heads(value_grads).astype(jnp.bfloat16), "ctx", scatter_dimension=1, tiled=True
        ).astype(jnp.float32),
    )
    query_sum = merge_heads(query_grads)
    bounds = ((0, img_member), (img_member, img_member + txt_member))
    grad_qkv_parts = []
    first_parts = []
    gain_terms = []
    for s in range(2):
        start_row, stop_row = bounds[s]
        unused, query_vjp = jax.vjp(
            lambda v, g: head_norm(v, g, QUERY_SCALE), projected[s][0], norm_gain[s, 0]
        )
        query_raw_grad, query_gain_grad = query_vjp(query_sum[:, start_row:stop_row])
        unused, key_vjp = jax.vjp(
            lambda v, g: head_norm(v, g, 1.0), projected[s][1], norm_gain[s, 1]
        )
        key_raw_grad, key_gain_grad = key_vjp(key_sum[:, start_row:stop_row])
        proj_grad = jnp.stack(
            [query_raw_grad, key_raw_grad, value_sum[:, start_row:stop_row]]
        ).astype(jnp.bfloat16)
        grad_qkv_parts.append(
            jnp.einsum("srd,csrf->cdf", first_in[s], proj_grad, preferred_element_type=jnp.float32)
        )
        first_parts.append(
            jnp.einsum("csrf,cdf->srd", proj_grad, qkv_back[s], preferred_element_type=jnp.float32)
        )
        gain_terms.append(jnp.stack([query_gain_grad, key_gain_grad]))
    first_grad = reduce_rows(first_parts[0], first_parts[1])
    input_grads = []
    mod_terms = []
    for s in range(2):
        unused, mod_vjp = jax.vjp(modulate, inputs[s], entry(s, 0), entry(s, 1))
        input_part, shift_part, scale_part = mod_vjp(first_grad[s])
        input_grads.append(mid_grad[s] + input_part)
        mod_terms.append(
            jnp.stack(
                [
                    shift_part[:, 0],
                    scale_part[:, 0],
                    gate_one[s],
                    shift_two[s],
                    scale_two[s],
                    gate_two[s],
                ],
                axis=1,
            )
        )
    mod_grad = lax.psum(jnp.stack(mod_terms).astype(jnp.bfloat16), ("ctx", "tp")).astype(
        jnp.float32
    )
    gain_grad = lax.psum(jnp.stack(gain_terms), ("shard", "ctx", "tp"))
    own_mod = lax.dynamic_slice_in_dim(
        mod_grad, lax.axis_index("tp") * local_feat, local_feat, axis=3
    ).astype(jnp.bfloat16)
    seq_count = cond_act.shape[0]
    cond_blocks = cond_act.reshape(seq_count, shard_count, ctx_count, owned_rows)
    cond_member = lax.dynamic_index_in_dim(
        cond_blocks, lax.axis_index("ctx"), axis=2, keepdims=False
    ).reshape(seq_count, shard_count * owned_rows)
    grad_mod_terms = jnp.einsum(
        "sd,tskf->tdkf", cond_member, own_mod, preferred_element_type=jnp.float32
    )
    grad_mod = lax.psum_scatter(
        grad_mod_terms.astype(jnp.bfloat16), "shard", scatter_dimension=1, tiled=True
    ).astype(jnp.float32)
    cond_part = jnp.einsum("tskf,tdkf->sd", own_mod, mod_all, preferred_element_type=jnp.float32)
    cond_total = lax.psum(cond_part, "tp")
    unused, silu_vjp = jax.vjp(jax.nn.silu, cond_float)
    grad_cond = silu_vjp(cond_total)[0]
    owned_grads = (
        lax.psum_scatter(
            jnp.stack(grad_qkv_parts), ("shard", "ctx"), scatter_dimension=2, tiled=True
        ),
        lax.psum_scatter(grad_outproj, ("shard", "ctx"), scatter_dimension=2, tiled=True),
        lax.psum_scatter(grad_up, ("shard", "ctx"), scatter_dimension=1, tiled=True),
        lax.psum_scatter(grad_down, ("shard", "ctx"), scatter_dimension=2, tiled=True),
    )
    factor = jnp.sqrt(threshold / jnp.maximum(peaks, threshold))
    columns = jnp.repeat(factor, head_dim)
    clipped = qkv_w[:, :2].astype(jnp.float32) * columns
    return (
        results[0],
        results[1],
        input_grads[0],
        input_grads[1],
        grad_cond,
        grad_mod,
        owned_grads[0],
        owned_grads[1],
        owned_grads[2],
        owned_grads[3],
        gain_grad,
        clipped,
        peaks,
    )


def solution(mesh):
    return jax.shard_map(
        local,
        mesh=mesh,
        in_specs=(
            P("shard", ("ctx", "tp"), None),
            P("shard", ("ctx", "tp"), None),
            P("shard", None),
            P("shard"),
            P(None, ("shard", "ctx"), None, "tp"),
            P(None, None, ("shard", "ctx"), "tp"),
            P(None, "tp", ("shard", "ctx")),
            P(None, ("shard", "ctx"), "tp"),
            P(None, "tp", ("shard", "ctx")),
            P(),
            P(),
            P("shard", ("ctx", "tp"), None),
            P("shard", ("ctx", "tp"), None),
        ),
        out_specs=(
            P("shard", ("ctx", "tp"), None),
            P("shard", ("ctx", "tp"), None),
            P("shard", ("ctx", "tp"), None),
            P("shard", ("ctx", "tp"), None),
            P("shard", None),
            P(None, ("shard", "ctx"), None, "tp"),
            P(None, None, ("shard", "ctx"), "tp"),
            P(None, "tp", ("shard", "ctx")),
            P(None, ("shard", "ctx"), "tp"),
            P(None, "tp", ("shard", "ctx")),
            P(),
            P(None, None, ("shard", "ctx"), "tp"),
            P("tp"),
        ),
        check_vma=False,
    )
```

profile of v0, /device:TPU:0, one launch (start us, length us, event | category | flops | bytes accessed | tf_op | source)
XLA Modules:
  0.0 3243.1 jit_solution(17155912777045053228)
XLA Ops:
  9.2 199.0 %all-gather.12.cloned.1.call-done = bf16[2,1536,6,384]{3,1,2,0:T(8,128)(2,1)} async-done(((bf16[2,192,6,384]{3,1,2,0:T(8,128)(2,1)}), bf16[2,1536,6,384]{3,1,2,0:T(8,128)(2,1)}) %all-gather.12.cloned.1.call-update) | async-done | bytes 14155792 | tf_op jit(solution)/shard_map/all_gather | solution.py:98
  233.3 83.5 %all-gather.16.cloned.1.call-done = bf16[2,3,1536,384]{3,2,1,0:T(8,128)(2,1)} async-done(((bf16[2,3,192,384]{3,2,1,0:T(8,128)(2,1)}), bf16[2,3,1536,384]{3,2,1,0:T(8,128)(2,1)}) %all-gather.16.cloned.1.call-update) | async-done | bytes 7077904 | tf_op jit(solution)/shard_map/all_gather | solution.py:90
  321.9 19.3 all-gather.14.cloned.1.call-done
  356.7 38.9 %all-gather.22.cloned.1.call-done = bf16[2,384,1536]{1,0,2:T(2,128)(2,1)} async-done(((bf16[2,384,192]{1,0,2:T(2,128)(2,1)}), bf16[2,384,1536]{1,0,2:T(2,128)(2,1)}) %all-gather.22.cloned.1.call-update) | async-done | bytes 2359312 | tf_op jit(solution)/shard_map/all_gather | solution.py:91
  412.6 40.1 %all-gather.18.cloned.1.call-done = bf16[3,1184,384]{2,1,0:T(8,128)(2,1)} async-done(((bf16[3,296,384]{2,1,0:T(8,128)(2,1)}), bf16[3,1184,384]{2,1,0:T(8,128)(2,1)}) %all-gather.18.cloned.1.call-update) | async-done | bytes 2727952 | tf_op jit(solution)/shard_map/all_gather | solution.py:122
  460.3 49.2 %all-gather.20.cloned.1.call-done = bf16[3,1184,384]{2,1,0:T(8,128)(2,1)} async-done(((bf16[3,296,384]{2,1,0:T(8,128)(2,1)}), bf16[3,1184,384]{2,1,0:T(8,128)(2,1)}) %all-gather.20.cloned.1.call-update) | async-done | bytes 2727952 | tf_op jit(solution)/shard_map/all_gather | solution.py:123
  518.5 53.4 %while.30 = (s32[]{:T(128)}, bf16[6,3,296,64]{2,3,1,0:T(8,128)(2,1)}, f32[6,3,296]{2,1,0:T(4,128)}, f32[6]{0:T(128)}, bf16[6,3,296,64]{2,3,1,0:T(8,128)(2,1)}, /...) while((s32[]{:T(128)}, ...), condition=%wide.region_12.13_spmd.clone, body=%wide.region_8.12_spmd.clone.sunk | while | flops 277630528 | bytes 13942453 | solution.py:149
  582.8 42.5 %reduce-scatter.8.cloned.1.call-done = f32[3,64,1536]{2,1,0:T(8,128)} async-done(((f32[3,256,1536]{2,1,0:T(8,128)}), f32[3,64,1536]{2,1,0:T(8,128)}) %reduce-scatter.8.cloned.1.call-update) | async-done | bytes 1179664 | tf_op jit(solution)/shard_map/reduce_scatter | solution.py:42
  637.4 127.8 %all-gather.28.cloned.1.call-done = bf16[2,1536,1536]{1,0,2:T(2,128)(2,1)} async-done(((bf16[2,1536,192]{1,0,2:T(2,128)(2,1)}), bf16[2,1536,1536]{1,0,2:T(2,128)(2,1)}) %all-gather.28.cloned.1.call-update) | async-done | bytes 9437200 | tf_op jit(solution)/shard_map/all_gather | solution.py:93
  765.2 19.1 fusion.191
  784.4 22.6 copy.359
  809.8 93.0 %all-gather.26.cloned.1.call-done = bf16[2,1536,1536]{2,1,0:T(8,128)(2,1)} async-done(((bf16[2,192,1536]{2,1,0:T(8,128)(2,1)}), bf16[2,1536,1536]{2,1,0:T(8,128)(2,1)}) %all-gather.26.cloned.1.call-update) | async-done | bytes 9437200 | tf_op jit(solution)/shard_map/all_gather | solution.py:92
  902.8 24.3 all-gather.24.cloned.1.call-done
  936.1 17.2 all-gather.30.cloned.1.call-done
  970.3 22.5 copy.364
  1020.9 22.0 reduce-scatter.12.cloned.1.call-done
  1047.5 34.0 %all-reduce.26.cloned.1.call-done = f32[3,40,1536]{2,0,1:T(4,128)} async-done(((f32[3,40,1536]{2,0,1:T(4,128)}), f32[3,40,1536]{2,0,1:T(4,128)}) %all-reduce.26.cloned.1.call-update) | async-done | bytes 737296
  1092.9 15.0 all-gather.32.cloned.1.call-done
  1111.2 73.6 %while.31 = (s32[]{:T(128)}, f32[6,3,296,64]{2,3,1,0:T(8,128)}, bf16[6,3,1184,64]{2,3,1,0:T(8,128)(2,1)}, bf16[6,3,1184,64]{2,3,1,0:T(8,128)(2,1)}, bf16[6,3,296...) while((s32[]{:T(128)}, f32[6,3,296,64]{2,3,1,0:T(8,128)}, ...), condition=%wide.region_29.30_spmd.clone, body=%wide.region_27.29_spmd.clone.sunk | while | flops 681308224 | bytes 36244180 | solution.py:265
  1237.5 161.6 %all-reduce.36.cloned.1.call-done = (bf16[3,1184,384]{2,1,0:T(8,128)(2,1)}, bf16[3,1184,384]{2,1,0:T(8,128)(2,1)}) async-done(((bf16[3,1184,384]{2,1,0:T(8,128)(2,1)}, bf16[3,1184,384]{2,1,0:T(8,128)(2,1)}), (bf16[3,1184,384]{2,1,0:T(8,128)(2,1)}, bf16[3,1184,384]{2,1,0:T(8,128)(2,1)})) %all-reduce.36.cloned.1.call-update) | async-done | bytes 5455888
  1491.7 41.6 %reduce-scatter.14.cloned.1.call-done = f32[3,64,1536]{2,1,0:T(8,128)} async-done(((f32[3,256,1536]{2,1,0:T(8,128)}), f32[3,64,1536]{2,1,0:T(8,128)}) %reduce-scatter.14.cloned.1.call-update) | async-done | bytes 1179664 | tf_op jit(solution)/shard_map/reduce_scatter | solution.py:42
  1538.9 44.8 %reduce-scatter.10.cloned.1.call-done = f32[3,64,1536]{2,1,0:T(8,128)} async-done(((f32[3,256,1536]{2,1,0:T(8,128)}), f32[3,64,1536]{2,1,0:T(8,128)}) %reduce-scatter.10.cloned.1.call-update) | async-done | bytes 1179664 | tf_op jit(solution)/shard_map/reduce_scatter | solution.py:42
  1592.1 14.6 pad_maximum_fusion.1
  1606.7 28.4 copy.329
  1635.6 45.5 %all-reduce.22.cloned.1.call-done = bf16[2,3,6,1536]{3,1,0,2:T(4,128)(2,1)} async-done(((bf16[2,3,6,1536]{3,1,0,2:T(4,128)(2,1)}), bf16[2,3,6,1536]{3,1,0,2:T(4,128)(2,1)}) %all-reduce.22.cloned.1.call-update) | async-done | bytes 110608 | tf_op jit(solution)/shard_map/psum | solution.py:322
  1748.7 21.6 copy.322
  1787.7 24.1 pmax.7
  1813.5 41.9 %psum.23 = f32[2,2,64]{2,1,0:T(2,128)} all-reduce(f32[2,2,64]{2,1,0:T(2,128)S(1)} %pad_maximum_fusion.13), channel_id=1, replica_groups=mesh['shard'=2,'ctx'=4,'tp'=4] {'shard','ctx','tp'}, use_global_device_ids=true, to_apply=%region_69.70 | all-reduce | flops 256 | bytes 2048 | tf_op jit(solution)/shard_map/psum | solution.py:325
  1855.4 399.6 %all-reduce.30.cloned.1.call-done = f32[2,1536,1536]{1,0,2:T(2,128)} async-done(((f32[2,1536,1536]{1,0,2:T(2,128)}), f32[2,1536,1536]{1,0,2:T(2,128)}) %all-reduce.30.cloned.1.call-update) | async-done | bytes 18874384
  2259.2 92.0 %all-reduce.28.cloned.1.call-done = bf16[2,384,6,384]{3,0,2,1:T(2,128)(2,1)} async-done(((bf16[2,384,6,384]{3,0,2,1:T(2,128)(2,1)}), bf16[2,384,6,384]{3,0,2,1:T(2,128)(2,1)}) %all-reduce.28.cloned.1.call-update) | async-done | bytes 3538960
  2356.1 566.9 %all-reduce.32.cloned.1.call-done = (f32[2,3,1536,384]{3,0,1,2:T(2,128)}, f32[2,384,1536]{1,0,2:T(2,128)}) async-done(((f32[2,3,1536,384]{3,0,1,2:T(2,128)}, f32[2,384,1536]{1,0,2:T(2,128)}), (f32[2,3,1536,384]{3,0,1,2:T(2,128)}, f32[2,384,1536]{1,0,2:T(2,128)})) %all-reduce.32.cloned.1.call-update) | async-done | bytes 18874384
  2928.5 307.5 %reduce-scatter.16.cloned.1.call-done = f32[2,192,1536]{2,1,0:T(8,128)} async-done(((f32[2,1536,1536]{2,1,0:T(8,128)}), f32[2,192,1536]{2,1,0:T(8,128)}) %reduce-scatter.16.cloned.1.call-update) | async-done | bytes 2359312 | tf_op jit(solution)/shard_map/reduce_scatter | solution.py:349
  (674 shorter events, 563.6 us)
Async XLA Ops:
  7.2 201.0 %copy-start.108 = (bf16[3,1536]{1,0:T(4,128)(2,1)S(1)}, bf16[3,1536]{1,0:T(4,128)(2,1)}, u32[]{:S(2)}) copy-start(bf16[3,1536]{1,0:T(4,128)(2,1)} %param.19) | copy-start | bytes 27652
  7.2 201.0 %all-gather.12.cloned.1.call-start = ((), (), s32[]{:S(2)}) async-start(), calls=%async_computation.5 | async-start | bytes 15925248 | tf_op jit(solution)/shard_map/all_gather | solution.py:98
  7.9 308.9 %all-gather.16.cloned.1.call-start = ((), (), s32[]{:S(2)}) async-start(), calls=%async_computation.7 | async-start | bytes 7962624 | tf_op jit(solution)/shard_map/all_gather | solution.py:90
  8.7 332.6 %all-gather.14.cloned.1.call-start = ((), (), s32[]{:S(2)}) async-start(), calls=%async_computation.6 | async-start | bytes 2949120 | tf_op jit(solution)/shard_map/all_gather | solution.py:35
  8.9 213.0 %copy-start.98 = (f32[3,64]{1,0:T(4,128)}, f32[3,64]{1,0:T(4,128)S(1)}, u32[]{:S(2)}) copy-start(f32[3,64]{1,0:T(4,128)S(1)} %broadcast_multiply_fusion.3) | copy-start | bytes 2308
  9.2 199.0 %copy-start.121 = (f32[3,64]{1,0:T(4,128)}, f32[3,64]{1,0:T(4,128)S(1)}, u32[]{:S(2)}) copy-start(f32[3,64]{1,0:T(4,128)S(1)} %fusion.97) | copy-start | bytes 2308
  9.2 212.6 %copy-start.117 = (f32[3,64]{1,0:T(4,128)}, f32[3,64]{1,0:T(4,128)S(1)}, u32[]{:S(2)}) copy-start(f32[3,64]{1,0:T(4,128)S(1)} %fusion.177) | copy-start | bytes 2308
  223.2 172.4 %all-gather.22.cloned.1.call-start = ((), (), s32[]{:S(2)}) async-start(), calls=%async_computation.10 | async-start | bytes 2654208 | tf_op jit(solution)/shard_map/all_gather | solution.py:91
  224.3 228.4 %all-gather.18.cloned.1.call-start = ((), (), s32[]{:S(2)}) async-start(), calls=%async_computation.8 | async-start | bytes 3409920 | tf_op jit(solution)/shard_map/all_gather | solution.py:122
  225.1 96.1 %copy-start.124 = (f32[384]{0:T(512)}, f32[384]{0:T(512)S(1)}, u32[]{:S(2)}) copy-start(f32[384]{0:T(512)S(1)} %mul.913) | copy-start | bytes 4612
  225.2 126.0 %copy-start.118 = (f32[384]{0:T(512)}, f32[384]{0:T(512)S(1)}, u32[]{:S(2)}) copy-start(f32[384]{0:T(512)S(1)} %mul.904) | copy-start | bytes 4612
  354.1 155.4 %all-gather.20.cloned.1.call-start = ((), (), s32[]{:S(2)}) async-start(), calls=%async_computation.9 | async-start | bytes 3409920 | tf_op jit(solution)/shard_map/all_gather | solution.py:123
  356.5 268.8 %reduce-scatter.8.cloned.1.call-start = ((), (), s32[]{:S(2)}) async-start(), calls=%async_computation.11 | async-start | bytes 5898240 | tf_op jit(solution)/shard_map/reduce_scatter | solution.py:42
  578.5 186.7 %all-gather.28.cloned.1.call-start = ((), (), s32[]{:S(2)}) async-start(), calls=%async_computation.14 | async-start | bytes 10616832 | tf_op jit(solution)/shard_map/all_gather | solution.py:93
  582.0 320.8 %all-gather.26.cloned.1.call-start = ((), (), s32[]{:S(2)}) async-start(), calls=%async_computation.13 | async-start | bytes 10616832 | tf_op jit(solution)/shard_map/all_gather | solution.py:92
  582.7 344.4 %all-gather.24.cloned.1.call-start = ((), (), s32[]{:S(2)}) async-start(), calls=%async_computation.12 | async-start | bytes 2949120 | tf_op jit(solution)/shard_map/all_gather | solution.py:35
  630.2 323.1 %all-gather.30.cloned.1.call-start = ((), (), s32[]{:S(2)}) async-start(), calls=%async_computation.16 | async-start | bytes 2949120 | tf_op jit(solution)/shard_map/all_gather | solution.py:35
  632.3 367.5 %all-reduce.24.cloned.1.call-start = ((), (), s32[]{:S(2)}) async-start(), calls=%async_computation.22 | async-start | bytes 1966080
  809.8 233.0 %reduce-scatter.12.cloned.1.call-start = ((), (), s32[]{:S(2)}) async-start(), calls=%async_computation.17 | async-start | bytes 5898240 | tf_op jit(solution)/shard_map/reduce_scatter | solution.py:42
  968.4 113.2 %all-reduce.26.cloned.1.call-start = ((), (), s32[]{:S(2)}) async-start(), calls=%async_computation.23 | async-start | bytes 1966080
  1020.4 87.5 %all-gather.32.cloned.1.call-start = ((), (), s32[]{:S(2)}) async-start(), calls=%async_computation.18 | async-start | bytes 2949120 | tf_op jit(solution)/shard_map/all_gather | solution.py:35
  1047.4 351.7 %all-reduce.36.cloned.1.call-start = ((), (), s32[]{:S(2)}) async-start(), calls=%async_computation.28 | async-start | bytes 10911744
  1203.0 280.0 %all-reduce.34.cloned.1.call-start = ((), (), s32[]{:S(2)}) async-start(), calls=%async_computation.27 | async-start | bytes 3932160
  1227.5 172.8 %copy-start.4 = (f32[3,256,384]{2,1,0:T(8,128)S(1)}, f32[3,256,384]{2,1,0:T(8,128)}, u32[]{:S(2)}) copy-start(f32[3,256,384]{2,1,0:T(8,128)} %copy-done.3) | copy-start | bytes 3538948
  1434.6 98.7 %reduce-scatter.14.cloned.1.call-start = ((), (), s32[]{:S(2)}) async-start(), calls=%async_computation.19 | async-start | bytes 5898240 | tf_op jit(solution)/shard_map/reduce_scatter | solution.py:42
  1448.3 135.4 %reduce-scatter.10.cloned.1.call-start = ((), (), s32[]{:S(2)}) async-start(), calls=%async_computation.15 | async-start | bytes 5898240 | tf_op jit(solution)/shard_map/reduce_scatter | solution.py:42
  1458.6 222.4 %all-reduce.22.cloned.1.call-start = ((), (), s32[]{:S(2)}) async-start(), calls=%async_computation.20 | async-start | bytes 294912 | tf_op jit(solution)/shard_map/psum | solution.py:322
  1592.1 662.9 %all-reduce.30.cloned.1.call-start = ((), (), s32[]{:S(2)}) async-start(), calls=%async_computation.25 | async-start | bytes 37748736
  1635.1 716.1 %all-reduce.28.cloned.1.call-start = ((), (), s32[]{:S(2)}) async-start(), calls=%async_computation.24 | async-start | bytes 7077888
  1711.4 1211.6 %all-reduce.32.cloned.1.call-start = ((), (), s32[]{:S(2)}) async-start(), calls=%async_computation.26 | async-start | bytes 37748736
  1770.3 1465.7 %reduce-scatter.16.cloned.1.call-start = ((), (), s32[]{:S(2)}) async-start(), calls=%async_computation.21 | async-start | bytes 21233664 | tf_op jit(solution)/shard_map/reduce_scatter | solution.py:349
  1811.8 445.6 %copy-start.146 = (f32[6]{0:T(128)}, f32[6]{0:T(128)S(1)}, u32[]{:S(2)}) copy-start(f32[6]{0:T(128)S(1)} %pmax.7) | copy-start | bytes 76
  (144 other events, 1996.9 us)
Sparse Core Ops, SparseCore 0:
  10.1 197.9 all-gather.11
  210.3 106.4 all-gather.15
  319.0 22.2 all-gather.13
  343.8 51.8 all-gather.21
  397.6 55.0 all-gather.17
  454.2 55.2 all-gather.19
  578.6 46.5 reduce-scatter.7
  627.9 137.2 all-gather.27
  767.4 135.4 all-gather.25
  904.8 22.2 all-gather.23
  929.2 24.0 all-gather.29
  956.1 35.9 all-reduce.23
  994.7 48.0 reduce-scatter.11
  1045.6 35.8 all-reduce.25
  1083.5 24.3 all-gather.31
  1203.1 195.9 all-reduce.35
  1434.7 48.2 all-reduce.33
  1485.3 47.9 reduce-scatter.13
  1535.8 47.8 reduce-scatter.9
  1592.2 88.8 all-reduce.21
  1685.1 569.7 all-reduce.29
  2257.8 93.4 all-reduce.27
  2355.5 567.4 all-reduce.31
  2927.3 308.7 reduce-scatter.15
where the time goes:
time: 3260 us; the launch traced here: 3240 us
  waiting for transfers between devices  2470 us (76%)
  local copies, waits for them, and re-layouts  293 us (9%)
  matrix products  216 us (7%)
  other arithmetic  127 us (4%)
  blocking collectives  110 us (3%)
    unnamed x31, waiting for transfers between devices  1260 us
    reduce_scatter x1, waiting for transfers between devices, local(): lax.psum_scatter(grad_up, ('shard', 'ctx'), scatter_dimension=1, tiled=True)  308 us
    all_gather x1, waiting for transfers between devices, local(): mod_all = lax.all_gather(mod_w, ('shard', 'ctx'), axis=1, tiled=True)  199 us
    reduce_scatter x4, waiting for transfers between devices, reduce_rows(): lax.psum_scatter(first, 'tp', scatter_dimension=1, tiled=True)  151 us
    all_gather x1, waiting for transfers between devices, local(): lax.all_gather(down_w, ('shard', 'ctx'), axis=2, tiled=True)  128 us
    unnamed x337, local copies, waits for them, and re-layouts  106 us
    all_gather x1, waiting for transfers between devices, local(): lax.all_gather(up_w, ('shard', 'ctx'), axis=1, tiled=True)  93 us
    all_gather x1, waiting for transfers between devices, local(): lax.all_gather(qkv_w, ('shard', 'ctx'), axis=2, tiled=True)  83.5 us
  transfers between devices with their start and end apart: 24, of which 23 were waited for; matrix products, arithmetic and copies ran while one was open for 13% of the time, Pallas kernels for 0%

commit v1 on v0

--- a/solution.py
+++ b/solution.py
@@ -5,6 +5,27 @@
 
 EPS = 1e-06
 QUERY_SCALE = 0.125
+
+
+def ring_gather(x, axis, dim):
+    peers, index, rows = (lax.axis_size(axis), lax.axis_index(axis), x.shape[dim])
+    upward = [(i, (i + 1) % peers) for i in range(peers)]
+    downward = [(i, (i - 1) % peers) for i in range(peers)]
+    out = jnp.zeros((*x.shape[:dim], peers * rows, *x.shape[dim + 1 :]), x.dtype)
+    out = lax.dynamic_update_slice_in_dim(out, x, index * rows, axis=dim)
+    from_left = from_right = x
+    middle = peers // 2
+    for step in range(1, middle + 1):
+        from_left = lax.ppermute(from_left, axis, upward)
+        out = lax.dynamic_update_slice_in_dim(
+            out, from_left, (index - step) % peers * rows, axis=dim
+        )
+        if step < peers - middle:
+            from_right = lax.ppermute(from_right, axis, downward)
+            out = lax.dynamic_update_slice_in_dim(
+                out, from_right, (index + step) % peers * rows, axis=dim
+            )
+    return out
 
 
 def layer_norm(values):
@@ -90,7 +111,7 @@
         lax.all_gather(qkv_w, ("shard", "ctx"), axis=2, tiled=True),
         lax.all_gather(o_w, ("shard", "ctx"), axis=2, tiled=True),
         lax.all_gather(up_w, ("shard", "ctx"), axis=1, tiled=True),
-        lax.all_gather(down_w, ("shard", "ctx"), axis=2, tiled=True),
+        ring_gather(down_w, ("shard", "ctx"), 2),
     )
     qkv_all, out_all, up_all, down_all = gathered
     cond_float = cond.astype(jnp.float32)

time: 3260 us -> 3450 us (1.058)
  local copies, waits for them, and re-layouts: 293 us -> 448 us
    ppermute x0 -> x7, waiting for transfers between devices: none -> 188 us  [the longest x3 160 us: ring_gather(): from_right = lax.ppermute(from_right, axis, downward)]
    unnamed x31, waiting for transfers between devices: 1260 us -> 1100 us
    dynamic_update_slice x0 -> x8, local copies, waits for them, and re-layouts: none -> 131 us  [the longest x4 64.9 us: ring_gather(): lax.dynamic_update_slice_in_dim(out, from_left, (index - step) % peers *...]
    unnamed x337 -> x348, local copies, waits for them, and re-layouts: 106 us -> 108 us
  transfers between devices with their start and end apart: 24 -> 31, of which waited for: 23 -> 26; matrix products, arithmetic and copies ran while one was open for 13% -> 19% of each run, Pallas kernels for 0% -> 0%
where the time goes in v1:
time: 3450 us; the launch traced here: 3430 us
  waiting for transfers between devices  2500 us (72%)
  local copies, waits for them, and re-layouts  448 us (13%)
  matrix products  216 us (6%)
  other arithmetic  127 us (4%)
  blocking collectives  110 us (3%)
    unnamed x31, waiting for transfers between devices  1100 us
    reduce_scatter x1, waiting for transfers between devices, local(): lax.psum_scatter(grad_up, ('shard', 'ctx'), scatter_dimension=1, tiled=True)  308 us
    all_gather x1, waiting for transfers between devices, local(): mod_all = lax.all_gather(mod_w, ('shard', 'ctx'), axis=1, tiled=True)  199 us
    ppermute x3, waiting for transfers between devices, ring_gather(): from_right = lax.ppermute(from_right, axis, downward)  160 us
    reduce_scatter x4, waiting for transfers between devices, reduce_rows(): lax.psum_scatter(first, 'tp', scatter_dimension=1, tiled=True)  151 us
    all_gather x1, waiting for transfers between devices, local(): lax.all_gather(down_w, ('shard', 'ctx'), axis=2, tiled=True)  128 us
    unnamed x348, local copies, waits for them, and re-layouts  108 us
    all_gather x1, waiting for transfers between devices, local(): lax.all_gather(up_w, ('shard', 'ctx'), axis=1, tiled=True)  92.6 us
  transfers between devices with their start and end apart: 31, of which 26 were waited for; matrix products, arithmetic and copies ran while one was open for 19% of the time, Pallas kernels for 0%

profile of v1, /device:TPU:0, one launch (start us, length us, event | category | flops | bytes accessed | tf_op | source)
XLA Modules:
  0.0 3431.2 jit_solution(982269765275253775)
XLA Ops:
  9.2 199.0 %all-gather.12.cloned.1.call-done = bf16[2,1536,6,384]{3,1,2,0:T(8,128)(2,1)} async-done(((bf16[2,192,6,384]{3,1,2,0:T(8,128)(2,1)}), bf16[2,1536,6,384]{3,1,2,0:T(8,128)(2,1)}) %all-gather.12.cloned.1.call-update) | async-done | bytes 14155792 | tf_op jit(solution)/shard_map/all_gather | solution.py:119
  233.7 83.2 %all-gather.16.cloned.1.call-done = bf16[2,3,1536,384]{3,2,1,0:T(8,128)(2,1)} async-done(((bf16[2,3,192,384]{3,2,1,0:T(8,128)(2,1)}), bf16[2,3,1536,384]{3,2,1,0:T(8,128)(2,1)}) %all-gather.16.cloned.1.call-update) | async-done | bytes 7077904 | tf_op jit(solution)/shard_map/all_gather | solution.py:111
  321.9 19.3 all-gather.14.cloned.1.call-done
  356.7 38.9 %all-gather.22.cloned.1.call-done = bf16[2,384,1536]{1,0,2:T(2,128)(2,1)} async-done(((bf16[2,384,192]{1,0,2:T(2,128)(2,1)}), bf16[2,384,1536]{1,0,2:T(2,128)(2,1)}) %all-gather.22.cloned.1.call-update) | async-done | bytes 2359312 | tf_op jit(solution)/shard_map/all_gather | solution.py:112
  412.7 40.0 %all-gather.18.cloned.1.call-done = bf16[3,1184,384]{2,1,0:T(8,128)(2,1)} async-done(((bf16[3,296,384]{2,1,0:T(8,128)(2,1)}), bf16[3,1184,384]{2,1,0:T(8,128)(2,1)}) %all-gather.18.cloned.1.call-update) | async-done | bytes 2727952 | tf_op jit(solution)/shard_map/all_gather | solution.py:143
  460.3 49.1 %all-gather.20.cloned.1.call-done = bf16[3,1184,384]{2,1,0:T(8,128)(2,1)} async-done(((bf16[3,296,384]{2,1,0:T(8,128)(2,1)}), bf16[3,1184,384]{2,1,0:T(8,128)(2,1)}) %all-gather.20.cloned.1.call-update) | async-done | bytes 2727952 | tf_op jit(solution)/shard_map/all_gather | solution.py:144
  518.6 53.4 %while.30 = (s32[]{:T(128)}, bf16[6,3,296,64]{2,3,1,0:T(8,128)(2,1)}, f32[6,3,296]{2,1,0:T(4,128)}, f32[6]{0:T(128)}, bf16[6,3,296,64]{2,3,1,0:T(8,128)(2,1)}, /...) while((s32[]{:T(128)}, ...), condition=%wide.region_12.13_spmd.clone, body=%wide.region_8.12_spmd.clone.sunk | while | flops 277630528 | bytes 13942953 | solution.py:170
  582.9 42.4 %reduce-scatter.8.cloned.1.call-done = f32[3,64,1536]{2,1,0:T(8,128)} async-done(((f32[3,256,1536]{2,1,0:T(8,128)}), f32[3,64,1536]{2,1,0:T(8,128)}) %reduce-scatter.8.cloned.1.call-update) | async-done | bytes 1179664 | tf_op jit(solution)/shard_map/reduce_scatter | solution.py:63
  637.7 127.6 %all-gather.30.cloned.1.call-done = bf16[2,1536,1536]{1,0,2:T(2,128)(2,1)} async-done(((bf16[2,1536,192]{1,0,2:T(2,128)(2,1)}), bf16[2,1536,1536]{1,0,2:T(2,128)(2,1)}) %all-gather.30.cloned.1.call-update) | async-done | bytes 9437200 | tf_op jit(solution)/shard_map/all_gather | solution.py:197
  765.3 19.5 fusion.189
  784.9 22.6 copy.389
  810.3 92.6 %all-gather.26.cloned.1.call-done = bf16[2,1536,1536]{2,1,0:T(8,128)(2,1)} async-done(((bf16[2,192,1536]{2,1,0:T(8,128)(2,1)}), bf16[2,1536,1536]{2,1,0:T(8,128)(2,1)}) %all-gather.26.cloned.1.call-update) | async-done | bytes 9437200 | tf_op jit(solution)/shard_map/all_gather | solution.py:113
  902.9 24.3 all-gather.24.cloned.1.call-done
  970.4 22.5 copy.394
  1020.8 22.4 reduce-scatter.12.cloned.1.call-done
  1049.3 32.8 all-reduce.26.cloned.1.call-done
  1111.5 73.7 %while.31 = (s32[]{:T(128)}, f32[6,3,296,64]{2,3,1,0:T(8,128)}, bf16[6,3,1184,64]{2,3,1,0:T(8,128)(2,1)}, bf16[6,3,1184,64]{2,3,1,0:T(8,128)(2,1)}, bf16[6,3,296...) while((s32[]{:T(128)}, f32[6,3,296,64]{2,3,1,0:T(8,128)}, ...), condition=%wide.region_29.30_spmd.clone, body=%wide.region_27.29_spmd.clone.sunk | while | flops 681308224 | bytes 36244172 | solution.py:286
  1208.9 88.5 %collective-permute-done.1 = bf16[2,1536,192]{1,2,0:T(8,128)(2,1)S(1)} collective-permute-done((bf16[2,1536,192]{1,2,0:T(8,128)(2,1)S(1)}, bf16[2,1536,192]{1,2,0:T(8,128)(2,1)S(1)}, u32[]{:S(2)}, u32[]{:S(2)}) %collective-permute-start.1) | collective-permute-done | bytes 1179680 | tf_op jit(solution)/shard_map/ppermute | solution.py:24
  1313.5 71.6 %collective-permute-done.3 = bf16[2,1536,192]{1,2,0:T(8,128)(2,1)} collective-permute-done((bf16[2,1536,192]{1,2,0:T(8,128)(2,1)S(1)}, bf16[2,1536,192]{1,2,0:T(8,128)(2,1)}, u32[]{:S(2)}, u32[]{:S(2)}) %collective-permute-start.3) | collective-permute-done | bytes 1179680 | tf_op jit(solution)/shard_map/ppermute | solution.py:24
  1444.7 17.5 dynamic_update_slice.49
  1499.4 17.5 dynamic_update_slice.52
  1679.9 41.6 %reduce-scatter.14.cloned.1.call-done = f32[3,64,1536]{2,1,0:T(8,128)} async-done(((f32[3,256,1536]{2,1,0:T(8,128)}), f32[3,64,1536]{2,1,0:T(8,128)}) %reduce-scatter.14.cloned.1.call-update) | async-done | bytes 1179664 | tf_op jit(solution)/shard_map/reduce_scatter | solution.py:63
  1727.1 44.8 %reduce-scatter.10.cloned.1.call-done = f32[3,64,1536]{2,1,0:T(8,128)} async-done(((f32[3,256,1536]{2,1,0:T(8,128)}), f32[3,64,1536]{2,1,0:T(8,128)}) %reduce-scatter.10.cloned.1.call-update) | async-done | bytes 1179664 | tf_op jit(solution)/shard_map/reduce_scatter | solution.py:63
  1794.9 28.4 copy.359
  1823.6 45.6 %all-reduce.22.cloned.1.call-done = bf16[2,3,6,1536]{3,1,0,2:T(4,128)(2,1)} async-done(((bf16[2,3,6,1536]{3,1,0,2:T(4,128)(2,1)}), bf16[2,3,6,1536]{3,1,0,2:T(4,128)(2,1)}) %all-reduce.22.cloned.1.call-update) | async-done | bytes 110608 | tf_op jit(solution)/shard_map/psum | solution.py:343
  1936.9 21.6 copy.352
  1975.9 24.1 pmax.7
  2001.7 41.9 %psum.23 = f32[2,2,64]{2,1,0:T(2,128)} all-reduce(f32[2,2,64]{2,1,0:T(2,128)S(1)} %pad_maximum_fusion.13), channel_id=1, replica_groups=mesh['shard'=2,'ctx'=4,'tp'=4] {'shard','ctx','tp'}, use_global_device_ids=true, to_apply=%region_69.70 | all-reduce | flops 256 | bytes 2048 | tf_op jit(solution)/shard_map/psum | solution.py:346
  2043.6 399.4 %all-reduce.30.cloned.1.call-done = f32[2,1536,1536]{1,0,2:T(2,128)} async-done(((f32[2,1536,1536]{1,0,2:T(2,128)}), f32[2,1536,1536]{1,0,2:T(2,128)}) %all-reduce.30.cloned.1.call-update) | async-done | bytes 18874384
  2447.3 92.0 %all-reduce.28.cloned.1.call-done = bf16[2,384,6,384]{3,0,2,1:T(2,128)(2,1)} async-done(((bf16[2,384,6,384]{3,0,2,1:T(2,128)(2,1)}), bf16[2,384,6,384]{3,0,2,1:T(2,128)(2,1)}) %all-reduce.28.cloned.1.call-update) | async-done | bytes 3538960
  2544.1 566.9 %all-reduce.32.cloned.1.call-done = (f32[2,3,1536,384]{3,0,1,2:T(2,128)}, f32[2,384,1536]{1,0,2:T(2,128)}) async-done(((f32[2,3,1536,384]{3,0,1,2:T(2,128)}, f32[2,384,1536]{1,0,2:T(2,128)}), (f32[2,3,1536,384]{3,0,1,2:T(2,128)}, f32[2,384,1536]{1,0,2:T(2,128)})) %all-reduce.32.cloned.1.call-update) | async-done | bytes 18874384
  3116.6 307.5 %reduce-scatter.16.cloned.1.call-done = f32[2,192,1536]{2,1,0:T(8,128)} async-done(((f32[2,1536,1536]{2,1,0:T(8,128)}), f32[2,192,1536]{2,1,0:T(8,128)}) %reduce-scatter.16.cloned.1.call-update) | async-done | bytes 2359312 | tf_op jit(solution)/shard_map/reduce_scatter | solution.py:370
  (715 shorter events, 766.3 us)
Async XLA Ops:
  7.2 201.0 %all-gather.12.cloned.1.call-start = ((), (), s32[]{:S(2)}) async-start(), calls=%async_computation.5 | async-start | bytes 15925248 | tf_op jit(solution)/shard_map/all_gather | solution.py:119
  7.9 308.9 %all-gather.16.cloned.1.call-start = ((), (), s32[]{:S(2)}) async-start(), calls=%async_computation.7 | async-start | bytes 7962624 | tf_op jit(solution)/shard_map/all_gather | solution.py:111
  8.7 332.6 %all-gather.14.cloned.1.call-start = ((), (), s32[]{:S(2)}) async-start(), calls=%async_computation.6 | async-start | bytes 2949120 | tf_op jit(solution)/shard_map/all_gather | solution.py:56
  223.2 172.4 %all-gather.22.cloned.1.call-start = ((), (), s32[]{:S(2)}) async-start(), calls=%async_computation.10 | async-start | bytes 2654208 | tf_op jit(solution)/shard_map/all_gather | solution.py:112
  224.3 228.4 %all-gather.18.cloned.1.call-start = ((), (), s32[]{:S(2)}) async-start(), calls=%async_computation.8 | async-start | bytes 3409920 | tf_op jit(solution)/shard_map/all_gather | solution.py:143
  354.1 155.4 %all-gather.20.cloned.1.call-start = ((), (), s32[]{:S(2)}) async-start(), calls=%async_computation.9 | async-start | bytes 3409920 | tf_op jit(solution)/shard_map/all_gather | solution.py:144
  356.4 268.9 %reduce-scatter.8.cloned.1.call-start = ((), (), s32[]{:S(2)}) async-start(), calls=%async_computation.11 | async-start | bytes 5898240 | tf_op jit(solution)/shard_map/reduce_scatter | solution.py:63
  578.6 186.7 %all-gather.30.cloned.1.call-start = ((), (), s32[]{:S(2)}) async-start(), calls=%async_computation.16 | async-start | bytes 10616832 | tf_op jit(solution)/shard_map/all_gather | solution.py:197
  582.1 320.8 %all-gather.26.cloned.1.call-start = ((), (), s32[]{:S(2)}) async-start(), calls=%async_computation.13 | async-start | bytes 10616832 | tf_op jit(solution)/shard_map/all_gather | solution.py:113
  582.8 344.3 %all-gather.24.cloned.1.call-start = ((), (), s32[]{:S(2)}) async-start(), calls=%async_computation.12 | async-start | bytes 2949120 | tf_op jit(solution)/shard_map/all_gather | solution.py:56
  630.3 323.1 %all-gather.28.cloned.1.call-start = ((), (), s32[]{:S(2)}) async-start(), calls=%async_computation.15 | async-start | bytes 2949120 | tf_op jit(solution)/shard_map/all_gather | solution.py:56
  632.4 367.6 %all-reduce.24.cloned.1.call-start = ((), (), s32[]{:S(2)}) async-start(), calls=%async_computation.22 | async-start | bytes 1966080
  810.3 232.9 %reduce-scatter.12.cloned.1.call-start = ((), (), s32[]{:S(2)}) async-start(), calls=%async_computation.17 | async-start | bytes 5898240 | tf_op jit(solution)/shard_map/reduce_scatter | solution.py:63
  968.5 113.7 %all-reduce.26.cloned.1.call-start = ((), (), s32[]{:S(2)}) async-start(), calls=%async_computation.23 | async-start | bytes 1966080
  1020.5 87.7 %all-gather.32.cloned.1.call-start = ((), (), s32[]{:S(2)}) async-start(), calls=%async_computation.18 | async-start | bytes 2949120 | tf_op jit(solution)/shard_map/all_gather | solution.py:56
  1047.7 538.8 %all-reduce.36.cloned.1.call-start = ((), (), s32[]{:S(2)}) async-start(), calls=%async_computation.28 | async-start | bytes 10911744
  1047.8 161.1 %collective-permute-start = (bf16[2,1536,192]{1,2,0:T(8,128)(2,1)}, bf16[2,1536,192]{1,2,0:T(8,128)(2,1)}, u32[]{:S(2)}, u32[]{:S(2)}) collective-permute-start(bf16[2,1536,192]{1,2,0:T(8,128)(2,1)} %param.25), channel_id=1, source_target_pairs={{0,4},{4,8},{8,12},{12,16},{16,20},{20,24},{24,28},{28,0},{1,5},{5... | collective-permute-start | bytes 3538952 | tf_op jit(solution)/shard_map/ppermute | solution.py:19
  1203.4 467.7 %all-reduce.34.cloned.1.call-start = ((), (), s32[]{:S(2)}) async-start(), calls=%async_computation.27 | async-start | bytes 3932160
  1204.7 92.8 %collective-permute-start.1 = (bf16[2,1536,192]{1,2,0:T(8,128)(2,1)S(1)}, bf16[2,1536,192]{1,2,0:T(8,128)(2,1)S(1)}, u32[]{:S(2)}, u32[]{:S(2)}) collective-permute-start(bf16[2,1536,192]{1,2,0:T(8,128)(2,1)S(1)} %copy-done.27), channel_id=1, source_target_pairs={{0,28},{4,0},{8,4},{12,8},{16,12},{20,16},{24,20},{28,24},{1,29},{... | collective-permute-start | bytes 3538952 | tf_op jit(solution)/shard_map/ppermute | solution.py:24
  1208.9 102.2 %collective-permute-start.2 = (bf16[2,1536,192]{1,2,0:T(8,128)(2,1)}, bf16[2,1536,192]{1,2,0:T(8,128)(2,1)S(1)}, u32[]{:S(2)}, u32[]{:S(2)}) collective-permute-start(bf16[2,1536,192]{1,2,0:T(8,128)(2,1)} %collective-permute-done), channel_id=1, source_target_pairs={{0,4},{4,8},{8,12},{12,16},{16,20},{20,24},{24,28},{28,0},{1,5},{5... | collective-permute-start | bytes 3538952 | tf_op jit(solution)/shard_map/ppermute | solution.py:19
  1298.4 86.7 %collective-permute-start.3 = (bf16[2,1536,192]{1,2,0:T(8,128)(2,1)S(1)}, bf16[2,1536,192]{1,2,0:T(8,128)(2,1)}, u32[]{:S(2)}, u32[]{:S(2)}) collective-permute-start(bf16[2,1536,192]{1,2,0:T(8,128)(2,1)S(1)} %collective-permute-done.1), channel_id=1, source_target_pairs={{0,28},{4,0},{8,4},{12,8},{16,12},{20,16},{24,20},{28,24},{1,29},{... | collective-permute-start | bytes 3538952 | tf_op jit(solution)/shard_map/ppermute | solution.py:24
  1311.1 88.8 %collective-permute-start.4 = (bf16[2,1536,192]{1,2,0:T(8,128)(2,1)S(1)}, bf16[2,1536,192]{1,2,0:T(8,128)(2,1)}, u32[]{:S(2)}, u32[]{:S(2)}) collective-permute-start(bf16[2,1536,192]{1,2,0:T(8,128)(2,1)S(1)} %collective-permute-done.2), channel_id=1, source_target_pairs={{0,4},{4,8},{8,12},{12,16},{16,20},{20,24},{24,28},{28,0},{1,5},{5... | collective-permute-start | bytes 3538952 | tf_op jit(solution)/shard_map/ppermute | solution.py:19
  1385.1 131.8 %collective-permute-start.5 = (bf16[2,1536,192]{1,2,0:T(8,128)(2,1)}, bf16[2,1536,192]{1,2,0:T(8,128)(2,1)}, u32[]{:S(2)}, u32[]{:S(2)}) collective-permute-start(bf16[2,1536,192]{1,2,0:T(8,128)(2,1)} %collective-permute-done.3), channel_id=1, source_target_pairs={{0,28},{4,0},{8,4},{12,8},{16,12},{20,16},{24,20},{28,24},{1,29},{... | collective-permute-start | bytes 3538952 | tf_op jit(solution)/shard_map/ppermute | solution.py:24
  1399.9 136.8 %collective-permute-start.6 = (bf16[2,1536,192]{1,2,0:T(8,128)(2,1)}, bf16[2,1536,192]{1,2,0:T(8,128)(2,1)}, u32[]{:S(2)}, u32[]{:S(2)}) collective-permute-start(bf16[2,1536,192]{1,2,0:T(8,128)(2,1)} %collective-permute-done.4), channel_id=1, source_target_pairs={{0,4},{4,8},{8,12},{12,16},{16,20},{20,24},{24,28},{28,0},{1,5},{5... | collective-permute-start | bytes 3538952 | tf_op jit(solution)/shard_map/ppermute | solution.py:19
  1621.9 99.6 %reduce-scatter.14.cloned.1.call-start = ((), (), s32[]{:S(2)}) async-start(), calls=%async_computation.19 | async-start | bytes 5898240 | tf_op jit(solution)/shard_map/reduce_scatter | solution.py:63
  1635.6 136.3 %reduce-scatter.10.cloned.1.call-start = ((), (), s32[]{:S(2)}) async-start(), calls=%async_computation.14 | async-start | bytes 5898240 | tf_op jit(solution)/shard_map/reduce_scatter | solution.py:63
  1646.1 223.1 %all-reduce.22.cloned.1.call-start = ((), (), s32[]{:S(2)}) async-start(), calls=%async_computation.20 | async-start | bytes 294912 | tf_op jit(solution)/shard_map/psum | solution.py:343
  1780.3 662.7 %all-reduce.30.cloned.1.call-start = ((), (), s32[]{:S(2)}) async-start(), calls=%async_computation.25 | async-start | bytes 37748736
  1823.4 716.0 %all-reduce.28.cloned.1.call-start = ((), (), s32[]{:S(2)}) async-start(), calls=%async_computation.24 | async-start | bytes 7077888
  1899.6 1211.5 %all-reduce.32.cloned.1.call-start = ((), (), s32[]{:S(2)}) async-start(), calls=%async_computation.26 | async-start | bytes 37748736
  1958.5 1465.6 %reduce-scatter.16.cloned.1.call-start = ((), (), s32[]{:S(2)}) async-start(), calls=%async_computation.21 | async-start | bytes 21233664 | tf_op jit(solution)/shard_map/reduce_scatter | solution.py:370
  2000.0 445.5 %copy-start.151 = (f32[6]{0:T(128)}, f32[6]{0:T(128)S(1)}, u32[]{:S(2)}) copy-start(f32[6]{0:T(128)S(1)} %pmax.7) | copy-start | bytes 76
  (156 other events, 3498.0 us)
Sparse Core Ops, SparseCore 0:
  10.1 197.9 all-gather.11
  210.3 106.4 all-gather.15
  319.0 22.2 all-gather.13
  343.8 51.8 all-gather.21
  397.6 55.0 all-gather.17
  454.2 55.2 all-gather.19
  578.7 46.5 reduce-scatter.7
  628.0 137.2 all-gather.29
  767.4 135.4 all-gather.25
  904.9 22.2 all-gather.23
  929.3 24.0 all-gather.27
  956.2 35.8 all-reduce.23
  994.7 48.4 reduce-scatter.11
  1046.0 36.1 all-reduce.25
  1084.1 24.0 all-gather.31
  1203.5 333.5 all-reduce.35
  1622.0 49.0 all-reduce.33
  1673.5 47.9 reduce-scatter.13
  1724.0 47.8 reduce-scatter.9
  1780.4 88.7 all-reduce.21
  1873.3 569.6 all-reduce.29
  2445.9 93.4 all-reduce.27
  2543.6 567.4 all-reduce.31
  3115.4 308.7 reduce-scatter.15
